TPU v7x, 32 devices: a whole 2x2x4 slice. The times are simulated.
32 devices in a mesh: rows: 16 (over z, y, x), grid: 2 (over core).
Axes of the slice: x: 2, y: 2, z: 4, core: 2. Of those that a mesh axis runs over, the one named last changes fastest.
Arguments:
- library: bfloat16 [8192, 4096], P('rows', 'grid'), may hold values from -6 to 6
- col_scale: float32 [4096], replicated, may hold values from 0.5 to 2
Outputs:
- updated: float32 [4096, 4096], P('rows', 'grid')
- reflectors: float32 [4096, 64], P('rows')
All inputs are finite; a program needn't handle non-finite values.
Results may differ from a plain program's by a relative error of at most 0.0003.
Values may be sent and summed in bfloat16 or wider, within the bound.
A program may use at most 128 MiB of HBM per device.

v0:
```python
import jax
import jax.numpy as jnp
from jax import lax
from jax.sharding import PartitionSpec as P

PANEL = 64


def broadcast(block, axis, source):
    block = jnp.where(lax.axis_index(axis) == source, block, jnp.zeros_like(block))
    return lax.psum(block, axis)


def reflect_panel(panel):
    size, width = panel.shape
    row_line = jnp.arange(size)
    col_line = jnp.arange(width)
    vectors = jnp.zeros((size, width), jnp.float32)
    factor = jnp.zeros((width, width), jnp.float32)

    def one_step(step, carry):
        work, vectors, factor = carry
        column = jnp.sum(jnp.where(col_line[None, :] == step, work, 0.0), axis=1)
        column = jnp.where(row_line >= step, column, 0.0)
        pivot = jnp.sum(jnp.where(row_line == step, column, 0.0))
        length = jnp.sqrt(jnp.sum(column * column))
        sign_factor = jnp.where(pivot >= 0.0, 1.0, -1.0)
        vector = column + jnp.where(row_line == step, sign_factor * length, 0.0)
        scale = 2.0 / jnp.sum(vector * vector)
        project = jnp.dot(vector, work, precision=lax.Precision.HIGHEST)
        work = work - scale * vector[:, None] * project[None, :]
        coupling = jnp.dot(vector, vectors, precision=lax.Precision.HIGHEST)
        column_t = -scale * jnp.dot(factor, coupling, precision=lax.Precision.HIGHEST)
        column_t = column_t + jnp.where(col_line == step, scale, 0.0)
        factor = jnp.where(col_line[None, :] == step, column_t[:, None], factor)
        vectors = jnp.where(col_line[None, :] == step, vector[:, None], vectors)
        return (work, vectors, factor)

    work, vectors, factor = lax.fori_loop(0, width, one_step, (panel, vectors, factor))
    return (vectors, factor)


def per_device(library, col_scale):
    rows_dev, col_block = library.shape
    count_rows = lax.axis_size("rows")
    count_grid = lax.axis_size("grid")
    columns = col_block * count_grid
    row_block = columns // count_rows
    total = rows_dev * count_rows
    grid_place = lax.axis_index("grid")
    rows_place = lax.axis_index("rows")
    own_scale = lax.dynamic_slice_in_dim(col_scale, grid_place * col_block, col_block)
    whole = lax.all_gather(library, "grid", axis=1, tiled=True)
    product = lax.dot_general(
        whole, library, (((0,), (0,)), ((), ())), preferred_element_type=jnp.float32
    )
    gram = lax.psum_scatter(
        product * (col_scale[:, None] * own_scale[None, :] / total),
        "rows",
        scatter_dimension=0,
        tiled=True,
    )
    head = gram[:, :PANEL]
    head = broadcast(head, "grid", 0)
    panel = lax.all_gather(head, "rows", axis=0, tiled=True)
    vectors, factor = reflect_panel(panel)
    own_vectors = lax.dynamic_slice_in_dim(vectors, rows_place * row_block, row_block, 0)
    partial_cross = jnp.dot(own_vectors.T, gram, precision=lax.Precision.HIGHEST)
    cross = lax.psum(partial_cross, "rows")
    mixed = jnp.dot(factor.T, cross, precision=lax.Precision.HIGHEST)
    updated = gram - jnp.dot(own_vectors, mixed, precision=lax.Precision.HIGHEST)
    return (updated, own_vectors)


def solution(mesh):
    return jax.shard_map(
        per_device,
        mesh=mesh,
        in_specs=(P("rows", "grid"), P()),
        out_specs=(P("rows", "grid"), P("rows", None)),
        check_vma=False,
    )
```

profile of v0, /device:TPU:0, one launch (start us, length us, event | category | flops | bytes accessed | tf_op | source)
XLA Modules:
  0.0 1997.8 jit_solution(2636637013112608751)
XLA Ops:
  8.0 17.9 all-gather.3.cloned.1.call-done
  26.0 17.6 multiply_multiply_fusion
  43.7 684.7 %reduce-scatter.2.cloned.1.call-done = f32[256,2048]{1,0:T(8,128)} async-done(((f32[4096,2048]{1,0:T(8,128)}), f32[256,2048]{1,0:T(8,128)}) %reduce-scatter.2.cloned.1.call-update) | async-done | bytes 2097168 | tf_op jit(solution)/shard_map/reduce_scatter | solution.py:57
  730.0 24.8 %all-reduce.3.cloned.1.call-done = f32[256,64]{1,0:T(8,128)} async-done(((f32[256,64]{1,0:T(8,128)}), f32[256,64]{1,0:T(8,128)}) %all-reduce.3.cloned.1.call-update) | async-done | bytes 65552 | tf_op jit(solution)/shard_map/psum | solution.py:11
  755.2 64.3 %all-gather.5.cloned.1.call-done = f32[4096,64]{1,0:T(8,128)} async-done(((f32[256,64]{1,0:T(8,128)}), f32[4096,64]{1,0:T(8,128)}) %all-gather.5.cloned.1.call-update) | async-done | bytes 1048592 | tf_op jit(solution)/shard_map/all_gather | solution.py:65
  819.4 1055.3 %while.19 = (s32[]{:T(128)}, f32[4096,64]{1,0:T(8,128)}, f32[4096,64]{1,0:T(8,128)}, f32[64,64]{1,0:T(8,128)S(1)}, s32[]{:T(128)}, /*index=5*/f32[]{:T(128)}, f32[]{:T(128)}, f32[]{:T(128)}, f32[]{:T(128)}, s32[]{:T(128)}) while((s32[]{:T(128)}, f32[4096,64]{1,0:T(8,128)}, f32[4096,64]{1,0:T(8,128)}, ...), condition=%wide.region_7.8_spmd.clone.clone, body=%wide.region_2.7_spmd.clone.clone.sunk | while | flops 8245573 | bytes 24332360 | solution.py:39
  827.6 3.9 multiply_subtract_fusion.2
  844.1 3.9 multiply_subtract_fusion.2
  860.6 3.9 multiply_subtract_fusion.2
  877.2 3.9 multiply_subtract_fusion.2
  910.2 3.9 multiply_subtract_fusion.2
  926.7 3.9 multiply_subtract_fusion.2
  943.2 3.9 multiply_subtract_fusion.2
  959.7 3.9 multiply_subtract_fusion.2
  976.3 3.9 multiply_subtract_fusion.2
  992.8 3.9 multiply_subtract_fusion.2
  1009.3 3.9 multiply_subtract_fusion.2
  1025.8 3.9 multiply_subtract_fusion.2
  1042.3 3.9 multiply_subtract_fusion.2
  1058.8 3.9 multiply_subtract_fusion.2
  1075.4 3.9 multiply_subtract_fusion.2
  1091.9 3.9 multiply_subtract_fusion.2
  1108.4 3.9 multiply_subtract_fusion.2
  1124.9 3.9 multiply_subtract_fusion.2
  1141.4 3.9 multiply_subtract_fusion.2
  1157.9 3.9 multiply_subtract_fusion.2
  1174.5 3.9 multiply_subtract_fusion.2
  1191.0 3.9 multiply_subtract_fusion.2
  1224.0 3.9 multiply_subtract_fusion.2
  1240.5 3.9 multiply_subtract_fusion.2
  1257.0 3.9 multiply_subtract_fusion.2
  1273.6 3.9 multiply_subtract_fusion.2
  1290.1 3.9 multiply_subtract_fusion.2
  1306.6 3.9 multiply_subtract_fusion.2
  1323.1 3.9 multiply_subtract_fusion.2
  1339.6 3.9 multiply_subtract_fusion.2
  1356.1 3.9 multiply_subtract_fusion.2
  1372.7 3.9 multiply_subtract_fusion.2
  1389.2 3.9 multiply_subtract_fusion.2
  1405.7 3.9 multiply_subtract_fusion.2
  1422.2 3.9 multiply_subtract_fusion.2
  1438.7 3.9 multiply_subtract_fusion.2
  1455.2 3.9 multiply_subtract_fusion.2
  1471.8 3.9 multiply_subtract_fusion.2
  1488.3 3.9 multiply_subtract_fusion.2
  1504.8 3.9 multiply_subtract_fusion.2
  1537.8 3.9 multiply_subtract_fusion.2
  1554.3 3.9 multiply_subtract_fusion.2
  1570.9 3.9 multiply_subtract_fusion.2
  1587.4 3.9 multiply_subtract_fusion.2
  1603.9 3.9 multiply_subtract_fusion.2
  1620.4 3.9 multiply_subtract_fusion.2
  1636.9 3.9 multiply_subtract_fusion.2
  1653.4 3.9 multiply_subtract_fusion.2
  1670.0 3.9 multiply_subtract_fusion.2
  1686.5 3.9 multiply_subtract_fusion.2
  1703.0 3.9 multiply_subtract_fusion.2
  1719.5 3.9 multiply_subtract_fusion.2
  1736.0 3.9 multiply_subtract_fusion.2
  1752.5 3.9 multiply_subtract_fusion.2
  1769.1 3.9 multiply_subtract_fusion.2
  1785.6 3.9 multiply_subtract_fusion.2
  1802.1 3.9 multiply_subtract_fusion.2
  1879.3 107.1 %all-reduce.5.cloned.1.call-done = f32[64,2048]{1,0:T(8,128)} async-done(((f32[64,2048]{1,0:T(8,128)}), f32[64,2048]{1,0:T(8,128)}) %all-reduce.5.cloned.1.call-update) | async-done | bytes 524304 | tf_op jit(solution)/shard_map/psum | solution.py:69
  (1122 shorter events, 705.0 us)
Async XLA Ops:
  7.2 18.8 copy-start.5
  7.2 18.8 all-gather.3.cloned.1.call-start
  7.9 720.5 %reduce-scatter.2.cloned.1.call-start = ((), (), s32[]{:S(2)}) async-start(), calls=%async_computation.2 | async-start | bytes 35651584 | tf_op jit(solution)/shard_map/reduce_scatter | solution.py:57
  43.6 711.2 %all-reduce.3.cloned.1.call-start = ((), (), s32[]{:S(2)}) async-start(), calls=%async_computation.3 | async-start | bytes 262144 | tf_op jit(solution)/shard_map/psum | solution.py:11
  730.0 89.4 %all-gather.5.cloned.1.call-start = ((), (), s32[]{:S(2)}) async-start(), calls=%async_computation.4 | async-start | bytes 2228224 | tf_op jit(solution)/shard_map/all_gather | solution.py:65
  754.9 1231.5 %all-reduce.5.cloned.1.call-start = ((), (), s32[]{:S(2)}) async-start(), calls=%async_computation.5 | async-start | bytes 1048576 | tf_op jit(solution)/shard_map/psum | solution.py:69
  834.2 8.8 copy-start
  850.7 8.8 copy-start
  867.2 8.8 copy-start
  883.7 8.8 copy-start
  900.3 8.8 copy-start
  916.8 8.8 copy-start
  933.3 8.8 copy-start
  949.8 8.8 copy-start
  966.3 8.8 copy-start
  982.8 8.8 copy-start
  999.4 8.8 copy-start
  1015.9 8.8 copy-start
  1032.4 8.8 copy-start
  1048.9 8.8 copy-start
  1065.4 8.8 copy-start
  1082.0 8.8 copy-start
  1098.5 8.8 copy-start
  1115.0 8.8 copy-start
  1131.5 8.8 copy-start
  1148.0 8.8 copy-start
  1164.5 8.8 copy-start
  1181.1 8.8 copy-start
  1197.6 8.8 copy-start
  1214.1 8.8 copy-start
  1230.6 8.8 copy-start
  1247.1 8.8 copy-start
  1263.6 8.8 copy-start
  1280.2 8.8 copy-start
  1296.7 8.8 copy-start
  1313.2 8.8 copy-start
  1329.7 8.8 copy-start
  1346.2 8.8 copy-start
  1362.7 8.8 copy-start
  1379.3 8.8 copy-start
  1395.8 8.8 copy-start
  1412.3 8.8 copy-start
  1428.8 8.8 copy-start
  1445.3 8.8 copy-start
  1461.8 8.8 copy-start
  1478.4 8.8 copy-start
  1494.9 8.8 copy-start
  1511.4 8.8 copy-start
  1527.9 8.8 copy-start
  1544.4 8.8 copy-start
  1560.9 8.8 copy-start
  1577.5 8.8 copy-start
  1594.0 8.8 copy-start
  1610.5 8.8 copy-start
  1627.0 8.8 copy-start
  1643.5 8.8 copy-start
  1676.6 8.8 copy-start
  1693.1 8.8 copy-start
  1709.6 8.8 copy-start
  1726.1 8.8 copy-start
  1825.2 8.8 copy-start
  1841.7 8.8 copy-start
  1858.2 8.8 copy-start
  1877.1 111.0 %copy-start.6 = (f32[256,64]{0,1:T(8,128)}, f32[256,64]{0,1:T(8,128)S(1)}, u32[]{:S(2)}) copy-start(f32[256,64]{0,1:T(8,128)S(1)} %constant_dynamic-slice_fusion) | copy-start | bytes 196612
  (201 other events, 491.5 us)
Sparse Core Ops, SparseCore 0:
  9.6 16.3 all-gather.2
  43.8 684.5 reduce-scatter.1
  731.3 23.5 all-reduce.2
  757.5 61.8 all-gather.4
  1879.5 106.9 all-reduce.4
where the time goes:
time: 2000 us
  waiting for transfers between devices  900 us (45%)
  other arithmetic  496 us (25%)
  matrix products  290 us (14%)
  local copies, waits for them, and re-layouts  158 us (8%)
  loops' own time  140 us (7%)
    reduce_scatter x1, waiting for transfers between devices, per_device(): lax.psum_scatter(product * (col_scale[:, None] * own_scale[None, :] / tot...  685 us
    sub x64, other arithmetic, one_step(): work = work - scale * vector[:, None] * project[None, :]  250 us
    dot_general x64, matrix products, one_step(): coupling = jnp.dot(vector, vectors, precision=lax.Precision.HIGHEST)  184 us
    while x512, local copies, waits for them, and re-layouts  156 us
    reduce_sum x64, other arithmetic, one_step(): column = jnp.sum(jnp.where(col_line[None, :] == step, work, 0.0), axis=1)  150 us
    another operation x1, loops' own time, reflect_panel(): lax.fori_loop(0, width, one_step, (panel, vectors, factor))  140 us
    psum x1, waiting for transfers between devices, per_device(): cross = lax.psum(partial_cross, 'rows')  107 us
    dot_general x64, matrix products, one_step(): project = jnp.dot(vector, work, precision=lax.Precision.HIGHEST)  72.2 us
  transfers between devices with their start and end apart: 5, of which 5 were waited for; matrix products, arithmetic and copies ran while one was open for 0% of the time, Pallas kernels for 0%

commit v1 on v0

--- a/solution.py
+++ b/solution.py
@@ -62,7 +62,20 @@
     )
     head = gram[:, :PANEL]
     head = broadcast(head, "grid", 0)
-    panel = lax.all_gather(head, "rows", axis=0, tiled=True)
+    ways, here, k = (lax.axis_size("rows"), lax.axis_index("rows"), head.shape[0])
+    lengths = [n * ways if d == 0 else n for d, n in enumerate(head.shape)]
+    panel = lax.dynamic_update_slice_in_dim(jnp.zeros(lengths, head.dtype), head, here * k, axis=0)
+    going_up = going_down = head
+    for far in range(1, ways // 2 + 1):
+        going_up = lax.ppermute(going_up, "rows", [(d, (d + 1) % ways) for d in range(ways)])
+        panel = lax.dynamic_update_slice_in_dim(panel, going_up, (here - far) % ways * k, axis=0)
+        if 2 * far < ways:
+            going_down = lax.ppermute(
+                going_down, "rows", [(d, (d - 1) % ways) for d in range(ways)]
+            )
+            panel = lax.dynamic_update_slice_in_dim(
+                panel, going_down, (here + far) % ways * k, axis=0
+            )
     vectors, factor = reflect_panel(panel)
     own_vectors = lax.dynamic_slice_in_dim(vectors, rows_place * row_block, row_block, 0)
     partial_cross = jnp.dot(own_vectors.T, gram, precision=lax.Precision.HIGHEST)

time: 2000 us -> 1810 us (0.905)
  local copies, waits for them, and re-layouts: 158 us -> 2.81 us
  starting transfers between devices: 0.38 us -> 39.4 us
  waiting for transfers between devices: 900 us -> 863 us
  other arithmetic: 496 us -> 475 us
    while x512 -> x0, local copies, waits for them, and re-layouts: 156 us -> none
    reduce_sum x64, other arithmetic: 150 us -> 39 us  [one_step(): column = jnp.sum(jnp.where(col_line[None, :] == step, work, 0.0), axis=1)]
    sub x64, other arithmetic: 250 us -> 341 us  [one_step(): work = work - scale * vector[:, None] * project[None, :]]
    all_gather x1 -> x0, waiting for transfers between devices: 64.3 us -> none  [per_device(): panel = lax.all_gather(head, 'rows', axis=0, tiled=True)]
    ppermute x0 -> x15, starting transfers between devices: none -> 39.2 us  [the longest x7 37.5 us: per_device(): lax.ppermute(going_down, 'rows', [(d, (d - 1) % ways) for d in range(ways)])]
    ppermute x0 -> x15, waiting for transfers between devices: none -> 31.4 us  [the longest x8 31.3 us: per_device(): lax.ppermute(going_up, 'rows', [(d, (d + 1) % ways) for d in range(ways)])]
  transfers between devices with their start and end apart: 5 -> 19, of which waited for: 5 -> 13; matrix products, arithmetic and copies ran while one was open for 0% -> 0% of each run, Pallas kernels for 0% -> 0%
where the time goes in v1:
time: 1810 us; the launch traced here: 1800 us
  waiting for transfers between devices  863 us (48%)
  other arithmetic  475 us (26%)
  matrix products  280 us (15%)
  loops' own time  129 us (7%)
  starting transfers between devices  39.4 us (2%)
    reduce_scatter x1, waiting for transfers between devices, per_device(): lax.psum_scatter(product * (col_scale[:, None] * own_scale[None, :] / tot...  685 us
    sub x64, other arithmetic, one_step(): work = work - scale * vector[:, None] * project[None, :]  341 us
    dot_general x64, matrix products, one_step(): coupling = jnp.dot(vector, vectors, precision=lax.Precision.HIGHEST)  174 us
    another operation x1, loops' own time, reflect_panel(): lax.fori_loop(0, width, one_step, (panel, vectors, factor))  129 us
    psum x1, waiting for transfers between devices, per_device(): cross = lax.psum(partial_cross, 'rows')  104 us
    dot_general x64, matrix products, one_step(): project = jnp.dot(vector, work, precision=lax.Precision.HIGHEST)  72.4 us
    reduce_sum x64, other arithmetic, one_step(): length = jnp.sqrt(jnp.sum(column * column))  43.1 us
    reduce_sum x64, other arithmetic, one_step(): scale = 2.0 / jnp.sum(vector * vector)  42.7 us
  transfers between devices with their start and end apart: 19, of which 13 were waited for; matrix products, arithmetic and copies ran while one was open for 0% of the time, Pallas kernels for 0%

profile of v1, /device:TPU:0, one launch (start us, length us, event | category | flops | bytes accessed | tf_op | source)
XLA Modules:
  0.0 1803.3 jit_solution(10774144682287939068)
XLA Ops:
  8.0 17.9 all-gather.2.cloned.1.call-done
  26.0 17.6 multiply_multiply_fusion
  43.6 684.7 %reduce-scatter.2.cloned.1.call-done = f32[256,2048]{1,0:T(8,128)} async-done(((f32[4096,2048]{1,0:T(8,128)}), f32[256,2048]{1,0:T(8,128)}) %reduce-scatter.2.cloned.1.call-update) | async-done | bytes 2097168 | tf_op jit(solution)/shard_map/reduce_scatter | solution.py:57
  730.3 23.9 %all-reduce.3.cloned.1.call-done = f32[256,64]{1,0:T(8,128)} async-done(((f32[256,64]{1,0:T(8,128)}), f32[256,64]{1,0:T(8,128)}) %all-reduce.3.cloned.1.call-update) | async-done | bytes 65552 | tf_op jit(solution)/shard_map/psum | solution.py:11
  764.1 5.5 collective-permute-start.3
  772.6 5.6 collective-permute-start.5
  781.3 5.6 collective-permute-start.7
  790.0 5.6 collective-permute-start.9
  798.5 5.6 collective-permute-start.11
  807.1 5.6 collective-permute-start.13
  816.8 8.5 collective-permute-done.14
  825.3 857.6 %while.19 = (s32[]{:T(128)}, f32[4096,64]{1,0:T(8,128)S(1)}, f32[4096,64]{1,0:T(8,128)}, f32[64,64]{1,0:T(8,128)S(1)}, s32[]{:T(128)}, /*index=5*/f32[]{:T(128)}, f32[]{:T(128)}, f32[]{:T(128)}, f32[]{:T(128)}, s32[]{:T(128)}) while((s32[]{:T(128)}, f32[4096,64]{1,0:T(8,128)S(1)}, f32[4096,64]{1,0:T(8,128)}, ...), condition=%wide.region_7.8_spmd.clone.clone, body=%wide.region_2.7_spmd.clone.clone.sunk | while | flops 8245573 | bytes 7555044 | solution.py:39
  843.7 5.4 multiply_subtract_fusion.2
  857.1 5.4 multiply_subtract_fusion.2
  870.6 5.4 multiply_subtract_fusion.2
  884.0 5.4 multiply_subtract_fusion.2
  897.5 5.4 multiply_subtract_fusion.2
  910.9 5.4 multiply_subtract_fusion.2
  924.4 5.4 multiply_subtract_fusion.2
  937.8 5.4 multiply_subtract_fusion.2
  951.3 5.4 multiply_subtract_fusion.2
  964.7 5.4 multiply_subtract_fusion.2
  978.2 5.4 multiply_subtract_fusion.2
  991.6 5.4 multiply_subtract_fusion.2
  1005.0 5.4 multiply_subtract_fusion.2
  1018.5 5.4 multiply_subtract_fusion.2
  1031.9 5.4 multiply_subtract_fusion.2
  1045.4 5.4 multiply_subtract_fusion.2
  1058.8 5.4 multiply_subtract_fusion.2
  1072.3 5.4 multiply_subtract_fusion.2
  1085.7 5.4 multiply_subtract_fusion.2
  1099.2 5.4 multiply_subtract_fusion.2
  1112.6 5.4 multiply_subtract_fusion.2
  1126.1 5.4 multiply_subtract_fusion.2
  1139.5 5.4 multiply_subtract_fusion.2
  1153.0 5.4 multiply_subtract_fusion.2
  1166.4 5.4 multiply_subtract_fusion.2
  1179.9 5.4 multiply_subtract_fusion.2
  1193.3 5.4 multiply_subtract_fusion.2
  1206.7 5.4 multiply_subtract_fusion.2
  1220.2 5.4 multiply_subtract_fusion.2
  1233.6 5.4 multiply_subtract_fusion.2
  1247.1 5.4 multiply_subtract_fusion.2
  1260.5 5.4 multiply_subtract_fusion.2
  1274.0 5.4 multiply_subtract_fusion.2
  1287.4 5.4 multiply_subtract_fusion.2
  1300.9 5.4 multiply_subtract_fusion.2
  1314.3 5.4 multiply_subtract_fusion.2
  1327.8 5.4 multiply_subtract_fusion.2
  1341.2 5.4 multiply_subtract_fusion.2
  1354.7 5.4 multiply_subtract_fusion.2
  1368.1 5.4 multiply_subtract_fusion.2
  1381.5 5.4 multiply_subtract_fusion.2
  1395.0 5.4 multiply_subtract_fusion.2
  1408.4 5.4 multiply_subtract_fusion.2
  1421.9 5.4 multiply_subtract_fusion.2
  1435.3 5.4 multiply_subtract_fusion.2
  1448.8 5.4 multiply_subtract_fusion.2
  1475.7 5.4 multiply_subtract_fusion.2
  1529.5 5.4 multiply_subtract_fusion.2
  1542.9 5.4 multiply_subtract_fusion.2
  1596.7 5.4 multiply_subtract_fusion.2
  1663.9 5.4 multiply_subtract_fusion.2
  1687.6 104.3 %all-reduce.5.cloned.1.call-done = f32[64,2048]{1,0:T(8,128)} async-done(((f32[64,2048]{1,0:T(8,128)}), f32[64,2048]{1,0:T(8,128)}) %all-reduce.5.cloned.1.call-update) | async-done | bytes 524304 | tf_op jit(solution)/shard_map/psum | solution.py:82
  (656 shorter events, 496.7 us)
Async XLA Ops:
  7.2 18.8 %copy-start.1 = (bf16[512,2048]{1,0:T(8,128)(2,1)S(1)}, bf16[512,2048]{1,0:T(8,128)(2,1)}, u32[]{:S(2)}) copy-start(bf16[512,2048]{1,0:T(8,128)(2,1)} %param.4) | copy-start | bytes 6291460
  7.2 0.9 copy-start.4
  7.2 18.8 %all-gather.2.cloned.1.call-start = ((), (), s32[]{:S(2)}) async-start(), calls=%async_computation.1 | async-start | bytes 6291456 | tf_op jit(solution)/shard_map/all_gather | solution.py:53
  7.9 720.4 %reduce-scatter.2.cloned.1.call-start = ((), (), s32[]{:S(2)}) async-start(), calls=%async_computation.2 | async-start | bytes 35651584 | tf_op jit(solution)/shard_map/reduce_scatter | solution.py:57
  43.6 710.7 %all-reduce.3.cloned.1.call-start = ((), (), s32[]{:S(2)}) async-start(), calls=%async_computation.3 | async-start | bytes 262144 | tf_op jit(solution)/shard_map/psum | solution.py:11
  729.9 1062.0 %all-reduce.5.cloned.1.call-start = ((), (), s32[]{:S(2)}) async-start(), calls=%async_computation.4 | async-start | bytes 1048576 | tf_op jit(solution)/shard_map/psum | solution.py:82
  754.2 5.8 copy-start.3
  754.2 9.8 collective-permute-start
  756.0 8.2 collective-permute-start.1
  764.0 8.6 collective-permute-start.2
  764.1 8.5 collective-permute-start.3
  772.6 8.7 collective-permute-start.4
  772.6 8.7 collective-permute-start.5
  781.3 8.7 collective-permute-start.6
  781.3 8.7 collective-permute-start.7
  790.0 8.6 collective-permute-start.8
  790.0 8.6 collective-permute-start.9
  798.5 8.6 collective-permute-start.10
  798.5 8.6 collective-permute-start.11
  807.1 9.6 collective-permute-start.12
  807.1 9.7 collective-permute-start.13
  816.8 8.6 collective-permute-start.14
  1683.0 2.4 copy-start
  1685.3 108.2 %copy-start.2 = (f32[256,64]{0,1:T(8,128)}, f32[256,64]{0,1:T(8,128)S(1)}, u32[]{:S(2)}) copy-start(f32[256,64]{0,1:T(8,128)S(1)} %constant_dynamic-slice_fusion) | copy-start | bytes 196612
Sparse Core Ops, SparseCore 0:
  9.6 16.3 all-gather.1
  43.7 684.5 reduce-scatter.1
  730.6 23.5 all-reduce.2
  1687.7 104.1 all-reduce.4
